TPU v7x, 32 devices: a whole 2x2x4 slice. The times are simulated.
32 devices in a mesh: grp: 2 (over x), row: 16 (over z, y, core).
Axes of the slice: x: 2, y: 2, z: 4, core: 2. Of those that a mesh axis runs over, the one named last changes fastest.
Arguments:
- latent: bfloat16 [4, 16, 48, 16], P('grp', 'row'), parts along dimension 0, may hold values from -70 to 70
- w_in: bfloat16 [27, 16, 512], replicated, may hold values from -0.3125 to 0.3125
- gain_in: float32 [512], replicated, may hold values from 0.25 to 1.75
- w_query: bfloat16 [512, 512], replicated, may hold values from -0.2298097 to 0.2298097
- w_key: bfloat16 [512, 512], replicated, may hold values from -1.45840774 to 1.45840774
- w_value: bfloat16 [512, 512], replicated, may hold values from -0.25 to 0.25
- w_out: bfloat16 [512, 512], replicated, may hold values from -0.25 to 0.25
- gain_up: float32 [512], replicated, may hold values from 0.25 to 1.75
- w_up: bfloat16 [27, 512, 512], P(None, 'row'), may hold values from -0.0546875 to 0.0546875
Outputs:
- decoded: bfloat16 [4, 32, 96, 512], P('grp', 'row'), parts along dimension 0
There are 2 independent parts, one for each index of `grp`. A program takes and returns all parts, laid end to end along the dimension named above; an argument that names none is the same for every part. Nothing has to cross between parts.
All inputs are finite; a program needn't handle non-finite values.
Results may differ from a plain program's by a relative error of at most 0.015.
Values may be sent and summed in bfloat16 or wider, within the bound.
No kernel may reach another device: no remote copies, remote signals or barrier semaphores. Data moves between devices by JAX's collectives and lax.ppermute only.
A program may use at most 128 MiB of HBM per device.

v0:
```python
import math
import jax
import jax.numpy as jnp
from jax import lax
from jax.sharding import PartitionSpec as P

GROUPS = 32
norm_eps = 1e-06


def extended(cells, sides, width):
    for axis, dim in sides:
        count = lax.axis_size(axis)
        ends = count - 1
        head = lax.slice_in_dim(cells, 0, width, axis=dim)
        tail = lax.slice_in_dim(cells, cells.shape[dim] - width, cells.shape[dim], axis=dim)
        cells = jnp.concatenate(
            [
                lax.ppermute(tail, axis, [(i, (i + 1) % count) for i in range(ends)]),
                cells,
                lax.ppermute(head, axis, [((i + 1) % count, i) for i in range(ends)]),
            ],
            axis=dim,
        )
    return cells


def pad_field(rimmed):
    spaced = jnp.pad(rimmed, ((0, 0), (0, 0), (1, 1), (0, 0)))
    first_frame = spaced[:1]
    return jnp.concatenate([first_frame, first_frame, spaced], axis=0)


def tap_windows(padded, frame_count, row_count, col_count):
    windows = []
    for frame_tap in range(3):
        for row_tap in range(3):
            for col_tap in range(3):
                windows.append(
                    padded[
                        frame_tap : frame_tap + frame_count,
                        row_tap : row_tap + row_count,
                        col_tap : col_tap + col_count,
                    ]
                )
    stacked = jnp.stack(windows, axis=3)
    return stacked.reshape(frame_count * row_count * col_count, -1)


def tap_products(padded, weight, frame_count, row_count, col_count):
    running = jnp.zeros((frame_count * row_count * col_count, weight.shape[2]), jnp.float32)
    for frame_tap in range(3):
        for row_tap in range(3):
            for col_tap in range(3):
                tap_index = (frame_tap * 3 + row_tap) * 3 + col_tap
                window = padded[
                    frame_tap : frame_tap + frame_count,
                    row_tap : row_tap + row_count,
                    col_tap : col_tap + col_count,
                ]
                window = window.reshape(frame_count * row_count * col_count, -1)
                running = running + jnp.dot(
                    window, weight[tap_index], preferred_element_type=jnp.float32
                )
    return running


def group_norm(volume, gain):
    grouped = volume.astype(jnp.float32).reshape(volume.shape[:3] + (GROUPS, -1))
    entry_count = (
        volume.shape[0]
        * volume.shape[1]
        * lax.axis_size("row")
        * volume.shape[2]
        * grouped.shape[4]
    )
    group_total = lax.psum(jnp.sum(grouped, axis=(0, 1, 2, 4)), "row")
    group_avg = group_total / entry_count
    centred = grouped - group_avg[:, None]
    variance = lax.psum(jnp.sum(centred * centred, axis=(0, 1, 2, 4)), "row") / entry_count
    normal_part = centred * lax.rsqrt(variance + norm_eps)[:, None]
    return normal_part.reshape(volume.shape) * gain


def per_device(latent, w_in, gain_in, w_query, w_key, w_value, w_out, gain_up, w_up):
    frame_count, row_count, col_count, _ = latent.shape
    chan_width = w_query.shape[0]
    rimmed = extended(latent, (("row", 1),), 1)
    first_out = jnp.dot(
        tap_windows(pad_field(rimmed), frame_count, row_count, col_count),
        w_in.reshape(-1, chan_width),
        preferred_element_type=jnp.float32,
    )
    first_out = first_out.astype(jnp.bfloat16).reshape(
        frame_count, row_count, col_count, chan_width
    )
    normed = group_norm(first_out, gain_in).astype(jnp.bfloat16)
    flat_rows = normed.reshape(-1, chan_width)
    queries = jnp.dot(flat_rows, w_query, preferred_element_type=jnp.float32).astype(jnp.bfloat16)
    queries = queries.reshape(frame_count, row_count * col_count, chan_width)
    score_scale = 1.0 / math.sqrt(chan_width)
    key_table = jnp.dot(flat_rows, w_key, preferred_element_type=jnp.float32).astype(jnp.bfloat16)
    value_table = jnp.dot(flat_rows, w_value, preferred_element_type=jnp.float32).astype(
        jnp.bfloat16
    )
    key_table = key_table.reshape(frame_count, row_count, col_count, chan_width)
    value_table = value_table.reshape(frame_count, row_count, col_count, chan_width)
    row_peak = jnp.full((frame_count, row_count * col_count), -jnp.inf, jnp.float32)
    denom = jnp.zeros((frame_count, row_count * col_count), jnp.float32)
    weighted = jnp.zeros((frame_count, row_count * col_count, chan_width), jnp.float32)
    scores = (
        jnp.einsum(
            "fqd,fkd->fqk",
            queries,
            lax.all_gather(key_table, "row", axis=1, tiled=True).reshape(
                frame_count, -1, chan_width
            ),
            preferred_element_type=jnp.float32,
        )
        * score_scale
    )
    new_peak = jnp.max(scores, axis=-1)
    correction = jnp.exp(row_peak - new_peak)
    expo = jnp.exp(scores - new_peak[..., None])
    denom = denom * correction + jnp.sum(expo, axis=-1)
    weighted = weighted * correction[..., None] + jnp.einsum(
        "fqk,fkd->fqd",
        expo.astype(jnp.bfloat16),
        lax.all_gather(value_table, "row", axis=1, tiled=True).reshape(frame_count, -1, chan_width),
        preferred_element_type=jnp.float32,
    )
    row_peak, denom, weighted = (new_peak, denom, weighted)
    attended = (weighted / denom[..., None]).astype(jnp.bfloat16).reshape(-1, chan_width)
    added = first_out.astype(jnp.float32).reshape(-1, chan_width) + jnp.dot(
        attended, w_out, preferred_element_type=jnp.float32
    )
    added = added.astype(jnp.bfloat16).reshape(frame_count, row_count, col_count, chan_width)
    full_up = lax.all_gather(w_up, "row", axis=1, tiled=True)
    upsampled = jnp.repeat(jnp.repeat(added, 2, axis=1), 2, axis=2)
    up_rimmed = extended(upsampled, (("row", 1),), 1)
    padded_up = pad_field(up_rimmed)
    running = tap_products(padded_up, full_up, frame_count, 2 * row_count, 2 * col_count)
    convolved = running.astype(jnp.bfloat16).reshape(
        frame_count, 2 * row_count, 2 * col_count, chan_width
    )
    return jax.nn.silu(group_norm(convolved, gain_up)).astype(jnp.bfloat16)


def solution(mesh):
    in_specs = (
        P("grp", "row", None, None),
        P(),
        P(),
        P(),
        P(),
        P(),
        P(),
        P(),
        P(None, "row", None),
    )
    out_specs = P("grp", "row", None, None)
    return jax.shard_map(
        per_device, mesh=mesh, in_specs=in_specs, out_specs=out_specs, check_vma=False
    )
```

profile of v0, /device:TPU:0, one launch (start us, length us, event | category | flops | bytes accessed | tf_op | source)
XLA Modules:
  0.0 361.8 jit_solution(4662353272731038480)
XLA Ops:
  6.5 1.4 collective-permute-start.1
  8.0 3.0 collective-permute-start
  16.7 35.5 %psum.28 = f32[32]{0:T(128)S(1)} all-reduce(f32[32]{0:T(128)S(1)} %reduce_sum.59), channel_id=1, replica_groups=mesh['grp'=2,'row'=16] {'row'}, use_global_device_ids=true, to_apply=%region_2.3 | all-reduce | flops 32 | bytes 256 | tf_op jit(solution)/shard_map/psum | solution.py:77
  52.5 29.5 %psum.29 = f32[32]{0:T(128)S(1)} all-reduce(f32[32]{0:T(128)S(1)} %reduce_sum.62), channel_id=1, replica_groups=mesh['grp'=2,'row'=16] {'row'}, use_global_device_ids=true, to_apply=%region_5.6 | all-reduce | flops 32 | bytes 256 | tf_op jit(solution)/shard_map/psum | solution.py:80
  83.9 1.9 convolution_convert_fusion.1
  86.5 1.3 convolution_convert_fusion.2
  87.8 33.0 %all-gather.6.cloned.1.call-done = bf16[2,16,48,512]{3,2,0,1:T(8,128)(2,1)} async-done(((bf16[2,1,48,512]{3,2,0,1:T(8,128)(2,1)}), bf16[2,16,48,512]{3,2,0,1:T(8,128)(2,1)}) %all-gather.6.cloned.1.call-update) | async-done | bytes 1572880 | tf_op jit(solution)/shard_map/all_gather | solution.py:129
  120.8 1.5 copy.34
  122.4 39.1 %all-gather.4.cloned.1.call-done = bf16[2,16,48,512]{3,2,0,1:T(8,128)(2,1)} async-done(((bf16[2,1,48,512]{3,2,0,1:T(8,128)(2,1)}), bf16[2,16,48,512]{3,2,0,1:T(8,128)(2,1)}) %all-gather.4.cloned.1.call-update) | async-done | bytes 1572880 | tf_op jit(solution)/shard_map/all_gather | solution.py:115
  161.5 1.5 copy.33
  164.7 1.3 collective-permute-start.3
  166.0 3.0 collective-permute-start.2
  170.5 2.1 pad_maximum_fusion.3
  173.6 2.3 pad_maximum_fusion.2
  175.9 97.0 %all-gather.8.cloned.1.call-done = bf16[27,512,512]{2,1,0:T(8,128)(2,1)} async-done(((bf16[27,32,512]{2,1,0:T(8,128)(2,1)}), bf16[27,512,512]{2,1,0:T(8,128)(2,1)}) %all-gather.8.cloned.1.call-update) | async-done | bytes 14155792 | tf_op jit(solution)/shard_map/all_gather | solution.py:138
  273.0 1.7 fusion.12
  274.7 2.2 convolution_add_fusion.25
  276.9 2.3 convolution_add_fusion.24
  279.2 1.6 convolution_add_fusion.23
  280.8 1.6 convolution_add_fusion.22
  282.4 1.6 convolution_add_fusion.21
  284.0 1.4 convolution_add_fusion.20
  293.3 30.8 %psum.30 = f32[32]{0:T(128)S(1)} all-reduce(f32[32]{0:T(128)S(1)} %reduce_sum.82), channel_id=1, replica_groups=mesh['grp'=2,'row'=16] {'row'}, use_global_device_ids=true, to_apply=%region_10.11 | all-reduce | flops 32 | bytes 256 | tf_op jit(solution)/shard_map/psum | solution.py:77
  324.6 29.5 %psum.31 = f32[32]{0:T(128)S(1)} all-reduce(f32[32]{0:T(128)S(1)} %reduce_sum.85), channel_id=1, replica_groups=mesh['grp'=2,'row'=16] {'row'}, use_global_device_ids=true, to_apply=%region_13.14 | all-reduce | flops 32 | bytes 256 | tf_op jit(solution)/shard_map/psum | solution.py:80
  (134 shorter events, 21.9 us)
Async XLA Ops:
  6.5 76.4 %copy-start = (bf16[512,512]{1,0:T(8,128)(2,1)S(1)}, bf16[512,512]{1,0:T(8,128)(2,1)}, u32[]{:S(2)}) copy-start(bf16[512,512]{1,0:T(8,128)(2,1)} %param.14) | copy-start | bytes 1572868
  6.5 157.8 %copy-start.15 = (bf16[512,512]{1,0:T(8,128)(2,1)S(1)}, bf16[512,512]{1,0:T(8,128)(2,1)}, u32[]{:S(2)}) copy-start(bf16[512,512]{1,0:T(8,128)(2,1)} %param.15) | copy-start | bytes 1572868
  6.5 114.3 %all-gather.6.cloned.1.call-start = ((), (), s32[]{:S(2)}) async-start(), calls=%async_computation.1 | async-start | bytes 1671168 | tf_op jit(solution)/shard_map/all_gather | solution.py:129
  6.5 4.5 %collective-permute-start.1 = (bf16[2,1,48,16]{2,3,1,0:T(8,128)(2,1)}, bf16[2,1,48,16]{2,3,1,0:T(8,128)(2,1)S(1)}, u32[]{:S(2)}, u32[]{:S(2)}) collective-permute-start(bf16[2,1,48,16]{2,3,1,0:T(8,128)(2,1)} %param.9), channel_id=1, source_target_pairs={{1,0},{2,1},{3,2},{4,3},{5,4},{6,5},{7,6},{8,7},{9,8},{10,9},{11,1... | collective-permute-start | bytes 9224 | tf_op jit(solution)/shard_map/ppermute | solution.py:21
  8.0 4.1 %collective-permute-start = (bf16[2,1,48,16]{2,3,0,1:T(8,128)(2,1)}, bf16[2,1,48,16]{2,3,0,1:T(8,128)(2,1)S(1)}, u32[]{:S(2)}, u32[]{:S(2)}) collective-permute-start(bf16[2,1,48,16]{2,3,0,1:T(8,128)(2,1)} %bitcast.310), channel_id=1, source_target_pairs={{0,1},{1,2},{2,3},{3,4},{4,5},{5,6},{6,7},{7,8},{8,9},{9,10},{10,1... | collective-permute-start | bytes 9224 | tf_op jit(solution)/shard_map/ppermute | solution.py:19
  83.8 77.6 %all-gather.4.cloned.1.call-start = ((), (), s32[]{:S(2)}) async-start(), calls=%async_computation | async-start | bytes 1671168 | tf_op jit(solution)/shard_map/all_gather | solution.py:115
  85.8 187.1 %all-gather.8.cloned.1.call-start = ((), (), s32[]{:S(2)}) async-start(), calls=%async_computation.2 | async-start | bytes 15040512 | tf_op jit(solution)/shard_map/all_gather | solution.py:138
  164.7 4.4 %collective-permute-start.3 = (bf16[2,1,96,512]{3,2,0,1:T(8,128)(2,1)S(1)}, bf16[2,1,96,512]{3,2,0,1:T(8,128)(2,1)S(1)}, u32[]{:S(2)}, u32[]{:S(2)}) collective-permute-start(bf16[2,1,96,512]{3,2,0,1:T(8,128)(2,1)S(1)} %slice.314), channel_id=1, source_target_pairs={{1,0},{2,1},{3,2},{4,3},{5,4},{6,5},{7,6},{8,7},{9,8},{10,9},{11,1... | collective-permute-start | bytes 589832 | tf_op jit(solution)/shard_map/ppermute | solution.py:21
  166.0 4.1 %collective-permute-start.2 = (bf16[2,1,96,512]{3,2,0,1:T(8,128)(2,1)S(1)}, bf16[2,1,96,512]{3,2,0,1:T(8,128)(2,1)S(1)}, u32[]{:S(2)}, u32[]{:S(2)}) collective-permute-start(bf16[2,1,96,512]{3,2,0,1:T(8,128)(2,1)S(1)} %slice.314), channel_id=1, source_target_pairs={{0,1},{1,2},{2,3},{3,4},{4,5},{5,6},{6,7},{7,8},{8,9},{9,10},{10,1... | collective-permute-start | bytes 589832 | tf_op jit(solution)/shard_map/ppermute | solution.py:19
  272.9 11.1 %copy-start.1 = (bf16[27,512,512]{2,1,0:T(8,128)(2,1)S(1)}, bf16[27,512,512]{2,1,0:T(8,128)(2,1)}, u32[]{:S(2)}) copy-start(bf16[27,512,512]{2,1,0:T(8,128)(2,1)} %all-gather.8.cloned.1.call-done) | copy-start | bytes 42467332
  272.9 12.5 %copy-start.11 = (bf16[2,2,96,512]{3,2,1,0:T(8,128)(2,1)S(1)}, bf16[2,2,96,512]{3,2,1,0:T(8,128)(2,1)}, u32[]{:S(2)}) copy-start(bf16[2,2,96,512]{3,2,1,0:T(8,128)(2,1)} %get-tuple-element.27) | copy-start | bytes 1179652
  272.9 12.9 %copy-start.9 = (bf16[2,2,96,512]{3,2,1,0:T(8,128)(2,1)S(1)}, bf16[2,2,96,512]{3,2,1,0:T(8,128)(2,1)}, u32[]{:S(2)}) copy-start(bf16[2,2,96,512]{3,2,1,0:T(8,128)(2,1)} %get-tuple-element.20) | copy-start | bytes 1179652
  273.0 13.3 %copy-start.13 = (bf16[2,2,96,512]{3,2,1,0:T(8,128)(2,1)S(1)}, bf16[2,2,96,512]{3,2,1,0:T(8,128)(2,1)}, u32[]{:S(2)}) copy-start(bf16[2,2,96,512]{3,2,1,0:T(8,128)(2,1)} %get-tuple-element.6) | copy-start | bytes 1179652
  273.0 13.7 %copy-start.12 = (bf16[2,2,96,512]{3,2,1,0:T(8,128)(2,1)S(1)}, bf16[2,2,96,512]{3,2,1,0:T(8,128)(2,1)}, u32[]{:S(2)}) copy-start(bf16[2,2,96,512]{3,2,1,0:T(8,128)(2,1)} %get-tuple-element.7) | copy-start | bytes 1179652
  273.0 14.0 %copy-start.10 = (bf16[2,2,96,512]{3,2,1,0:T(8,128)(2,1)S(1)}, bf16[2,2,96,512]{3,2,1,0:T(8,128)(2,1)}, u32[]{:S(2)}) copy-start(bf16[2,2,96,512]{3,2,1,0:T(8,128)(2,1)} %get-tuple-element.8) | copy-start | bytes 1179652
  273.0 14.4 %copy-start.8 = (bf16[2,2,96,512]{3,2,1,0:T(8,128)(2,1)S(1)}, bf16[2,2,96,512]{3,2,1,0:T(8,128)(2,1)}, u32[]{:S(2)}) copy-start(bf16[2,2,96,512]{3,2,1,0:T(8,128)(2,1)} %get-tuple-element.9) | copy-start | bytes 1179652
  276.9 10.9 %copy-start.7 = (bf16[2,2,96,512]{3,2,1,0:T(8,128)(2,1)S(1)}, bf16[2,2,96,512]{3,2,1,0:T(8,128)(2,1)}, u32[]{:S(2)}) copy-start(bf16[2,2,96,512]{3,2,1,0:T(8,128)(2,1)} %get-tuple-element.10) | copy-start | bytes 1179652
  279.2 8.9 %copy-start.6 = (bf16[2,2,96,512]{3,2,1,0:T(8,128)(2,1)S(1)}, bf16[2,2,96,512]{3,2,1,0:T(8,128)(2,1)}, u32[]{:S(2)}) copy-start(bf16[2,2,96,512]{3,2,1,0:T(8,128)(2,1)} %get-tuple-element.11) | copy-start | bytes 1179652
  280.8 7.7 %copy-start.5 = (bf16[2,2,96,512]{3,2,1,0:T(8,128)(2,1)S(1)}, bf16[2,2,96,512]{3,2,1,0:T(8,128)(2,1)}, u32[]{:S(2)}) copy-start(bf16[2,2,96,512]{3,2,1,0:T(8,128)(2,1)} %get-tuple-element.12) | copy-start | bytes 1179652
  282.4 6.5 %copy-start.4 = (bf16[2,2,96,512]{3,2,1,0:T(8,128)(2,1)S(1)}, bf16[2,2,96,512]{3,2,1,0:T(8,128)(2,1)}, u32[]{:S(2)}) copy-start(bf16[2,2,96,512]{3,2,1,0:T(8,128)(2,1)} %get-tuple-element.13) | copy-start | bytes 1179652
  284.0 5.3 %copy-start.3 = (bf16[2,2,96,512]{3,2,1,0:T(8,128)(2,1)S(1)}, bf16[2,2,96,512]{3,2,1,0:T(8,128)(2,1)}, u32[]{:S(2)}) copy-start(bf16[2,2,96,512]{3,2,1,0:T(8,128)(2,1)} %get-tuple-element.5) | copy-start | bytes 1179652
  285.5 4.3 %copy-start.2 = (bf16[2,2,96,512]{3,2,1,0:T(8,128)(2,1)S(1)}, bf16[2,2,96,512]{3,2,1,0:T(8,128)(2,1)}, u32[]{:S(2)}) copy-start(bf16[2,2,96,512]{3,2,1,0:T(8,128)(2,1)} %get-tuple-element.19) | copy-start | bytes 1179652
  288.5 4.2 %copy-start.14 = (bf16[2,2,96,512]{3,2,1,0:T(8,128)(2,1)S(1)}, bf16[2,2,96,512]{3,2,1,0:T(8,128)(2,1)}, u32[]{:S(2)}) copy-start(bf16[2,2,96,512]{3,2,1,0:T(8,128)(2,1)} %get-tuple-element.14) | copy-start | bytes 1179652
  288.9 65.4 %copy-start.16 = (f32[512]{0:T(512)S(1)}, f32[512]{0:T(512)}, u32[]{:S(2)}) copy-start(f32[512]{0:T(512)} %param.16) | copy-start | bytes 6148
Sparse Core Ops, SparseCore 0:
  83.9 36.8 all-gather.5
  123.1 38.2 all-gather.3
  163.7 109.2 all-gather.7
where the time goes:
time: 362 us
  waiting for transfers between devices  172 us (48%)
  blocking collectives  125 us (35%)
  matrix products  26.3 us (7%)
  between operations  13.7 us (4%)
  other arithmetic  9.18 us (3%)
  starting transfers between devices  8.87 us (2%)
  local copies, waits for them, and re-layouts  6.63 us (2%)
    all_gather x1, waiting for transfers between devices, per_device(): full_up = lax.all_gather(w_up, 'row', axis=1, tiled=True)  97 us
    psum x2, blocking collectives, group_norm(): group_total = lax.psum(jnp.sum(grouped, axis=(0, 1, 2, 4)), 'row')  66.3 us
    psum x2, blocking collectives, group_norm(): lax.psum(jnp.sum(centred * centred, axis=(0, 1, 2, 4)), 'row') / entry_count  59 us
    all_gather x1, waiting for transfers between devices, per_device(): lax.all_gather(key_table, 'row', axis=1, tiled=True)  39.1 us
    all_gather x1, waiting for transfers between devices, per_device(): lax.all_gather(value_table, 'row', axis=1, tiled=True)  33 us
    dot_general x27, matrix products, tap_products(): jnp.dot(window, weight[tap_index], preferred_element_type=jnp.float32)  19.7 us
  transfers between devices with their start and end apart: 7, of which 5 were waited for; matrix products, arithmetic and copies ran while one was open for 4% of the time, Pallas kernels for 0%

commit v1 on v0

--- a/solution.py
+++ b/solution.py
@@ -6,6 +6,19 @@
 
 GROUPS = 32
 norm_eps = 1e-06
+
+
+def gather_around(x, axis, dim):
+    ways = lax.axis_size(axis)
+    up = [(d, (d + 1) % ways) for d in range(ways)]
+    down = [(d, (d - 1) % ways) for d in range(ways)]
+    earlier, later = ([x], [x])
+    for _ in range(ways // 2):
+        earlier.append(lax.ppermute(earlier[-1], axis, up))
+    for _ in range((ways - 1) // 2):
+        later.append(lax.ppermute(later[-1], axis, down))
+    line = jnp.concatenate([*earlier[::-1], *later[1:]], axis=dim)
+    return jnp.roll(line, (lax.axis_index(axis) - ways // 2) * x.shape[dim], axis=dim)
 
 
 def extended(cells, sides, width):
@@ -126,7 +139,7 @@
     weighted = weighted * correction[..., None] + jnp.einsum(
         "fqk,fkd->fqd",
         expo.astype(jnp.bfloat16),
-        lax.all_gather(value_table, "row", axis=1, tiled=True).reshape(frame_count, -1, chan_width),
+        gather_around(value_table, "row", 1).reshape(frame_count, -1, chan_width),
         preferred_element_type=jnp.float32,
     )
     row_peak, denom, weighted = (new_peak, denom, weighted)

time: 362 us -> 325 us (0.90)
  waiting for transfers between devices: 172 us -> 107 us
  starting transfers between devices: 8.87 us -> 40.5 us
    all_gather x1, waiting for transfers between devices: 39.1 us -> 0.02 us  [per_device(): lax.all_gather(key_table, 'row', axis=1, tiled=True)]
    all_gather x1 -> x0, waiting for transfers between devices: 33 us -> none  [per_device(): lax.all_gather(value_table, 'row', axis=1, tiled=True)]
    ppermute x0 -> x15, starting transfers between devices: none -> 31.5 us  [the longest x7 31.5 us: gather_around(): later.append(lax.ppermute(later[-1], axis, down))]
    ppermute x0 -> x15, waiting for transfers between devices: none -> 29.1 us  [the longest x8 26 us: gather_around(): earlier.append(lax.ppermute(earlier[-1], axis, up))]
    all_gather x1, waiting for transfers between devices: 97 us -> 75.1 us  [per_device(): full_up = lax.all_gather(w_up, 'row', axis=1, tiled=True)]
  transfers between devices with their start and end apart: 7 -> 21, of which waited for: 5 -> 13; matrix products, arithmetic and copies ran while one was open for 4% -> 3% of each run, Pallas kernels for 0% -> 0%
where the time goes in v1:
time: 325 us
  blocking collectives  125 us (38%)
  waiting for transfers between devices  107 us (33%)
  starting transfers between devices  40.5 us (12%)
  matrix products  22.9 us (7%)
  between operations  14.4 us (4%)
  other arithmetic  9.19 us (3%)
  local copies, waits for them, and re-layouts  5.75 us (2%)
    all_gather x1, waiting for transfers between devices, per_device(): full_up = lax.all_gather(w_up, 'row', axis=1, tiled=True)  75.1 us
    psum x2, blocking collectives, group_norm(): group_total = lax.psum(jnp.sum(grouped, axis=(0, 1, 2, 4)), 'row')  66.3 us
    psum x2, blocking collectives, group_norm(): lax.psum(jnp.sum(centred * centred, axis=(0, 1, 2, 4)), 'row') / entry_count  59 us
    ppermute x7, starting transfers between devices, gather_around(): later.append(lax.ppermute(later[-1], axis, down))  31.5 us
    ppermute x8, waiting for transfers between devices, gather_around(): earlier.append(lax.ppermute(earlier[-1], axis, up))  26 us
    dot_general x27, matrix products, tap_products(): jnp.dot(window, weight[tap_index], preferred_element_type=jnp.float32)  19.1 us
  transfers between devices with their start and end apart: 21, of which 13 were waited for; matrix products, arithmetic and copies ran while one was open for 3% of the time, Pallas kernels for 0%

profile of v1, /device:TPU:0, one launch (start us, length us, event | category | flops | bytes accessed | tf_op | source)
XLA Modules:
  0.0 324.8 jit_solution(5126789945253491930)
XLA Ops:
  8.0 3.0 collective-permute-start
  16.7 35.5 %psum.28 = f32[32]{0:T(128)S(1)} all-reduce(f32[32]{0:T(128)S(1)} %reduce_sum.59), channel_id=1, replica_groups=mesh['grp'=2,'row'=16] {'row'}, use_global_device_ids=true, to_apply=%region_2.3 | all-reduce | flops 32 | bytes 256 | tf_op jit(solution)/shard_map/psum | solution.py:90
  52.6 29.5 %psum.29 = f32[32]{0:T(128)S(1)} all-reduce(f32[32]{0:T(128)S(1)} %reduce_sum.62), channel_id=1, replica_groups=mesh['grp'=2,'row'=16] {'row'}, use_global_device_ids=true, to_apply=%region_5.6 | all-reduce | flops 32 | bytes 256 | tf_op jit(solution)/shard_map/psum | solution.py:93
  84.9 6.7 %collective-permute-done.2 = bf16[2,1,48,512]{3,2,0,1:T(8,128)(2,1)S(1)} collective-permute-done((bf16[2,1,48,512]{3,2,0,1:T(8,128)(2,1)S(1)}, bf16[2,1,48,512]{3,2,0,1:T(8,128)(2,1)S(1)}, u32[]{:S(2)}, u32[]{:S(2)}) %collective-permute-start.2) | collective-permute-done | bytes 98336 | tf_op jit(solution)/shard_map/ppermute | solution.py:17
  91.6 4.4 %collective-permute-start.10 = (bf16[2,1,48,512]{3,2,0,1:T(8,128)(2,1)S(1)}, bf16[2,1,48,512]{3,2,0,1:T(8,128)(2,1)S(1)}, u32[]{:S(2)}, u32[]{:S(2)}) collective-permute-start(bf16[2,1,48,512]{3,2,0,1:T(8,128)(2,1)S(1)} %bitcast.301), channel_id=1, source_target_pairs={{0,15},{1,0},{2,1},{3,2},{4,3},{5,4},{6,5},{7,6},{8,7},{9,8},{10,9... | collective-permute-start | bytes 294920 | tf_op jit(solution)/shard_map/ppermute | solution.py:19
  96.1 3.1 collective-permute-done.3
  99.2 4.4 %collective-permute-start.11 = (bf16[2,1,48,512]{3,2,0,1:T(8,128)(2,1)S(1)}, bf16[2,1,48,512]{3,2,0,1:T(8,128)(2,1)S(1)}, u32[]{:S(2)}, u32[]{:S(2)}) collective-permute-start(bf16[2,1,48,512]{3,2,0,1:T(8,128)(2,1)S(1)} %collective-permute-done.10), channel_id=1, source_target_pairs={{0,15},{1,0},{2,1},{3,2},{4,3},{5,4},{6,5},{7,6},{8,7},{9,8},{10,9... | collective-permute-start | bytes 294920 | tf_op jit(solution)/shard_map/ppermute | solution.py:19
  103.7 2.3 collective-permute-done.4
  106.0 4.5 %collective-permute-start.12 = (bf16[2,1,48,512]{3,2,0,1:T(8,128)(2,1)S(1)}, bf16[2,1,48,512]{3,2,0,1:T(8,128)(2,1)S(1)}, u32[]{:S(2)}, u32[]{:S(2)}) collective-permute-start(bf16[2,1,48,512]{3,2,0,1:T(8,128)(2,1)S(1)} %collective-permute-done.11), channel_id=1, source_target_pairs={{0,15},{1,0},{2,1},{3,2},{4,3},{5,4},{6,5},{7,6},{8,7},{9,8},{10,9... | collective-permute-start | bytes 294920 | tf_op jit(solution)/shard_map/ppermute | solution.py:19
  110.5 4.2 %collective-permute-done.5 = bf16[2,1,48,512]{3,2,0,1:T(8,128)(2,1)S(1)} collective-permute-done((bf16[2,1,48,512]{3,2,0,1:T(8,128)(2,1)S(1)}, bf16[2,1,48,512]{3,2,0,1:T(8,128)(2,1)S(1)}, u32[]{:S(2)}, u32[]{:S(2)}) %collective-permute-start.5) | collective-permute-done | bytes 98336 | tf_op jit(solution)/shard_map/ppermute | solution.py:17
  114.7 4.4 %collective-permute-start.13 = (bf16[2,1,48,512]{3,2,0,1:T(8,128)(2,1)S(1)}, bf16[2,1,48,512]{3,2,0,1:T(8,128)(2,1)S(1)}, u32[]{:S(2)}, u32[]{:S(2)}) collective-permute-start(bf16[2,1,48,512]{3,2,0,1:T(8,128)(2,1)S(1)} %collective-permute-done.12), channel_id=1, source_target_pairs={{0,15},{1,0},{2,1},{3,2},{4,3},{5,4},{6,5},{7,6},{8,7},{9,8},{10,9... | collective-permute-start | bytes 294920 | tf_op jit(solution)/shard_map/ppermute | solution.py:19
  119.1 2.5 collective-permute-done.6
  121.6 4.4 %collective-permute-start.14 = (bf16[2,1,48,512]{3,2,0,1:T(8,128)(2,1)S(1)}, bf16[2,1,48,512]{3,2,0,1:T(8,128)(2,1)S(1)}, u32[]{:S(2)}, u32[]{:S(2)}) collective-permute-start(bf16[2,1,48,512]{3,2,0,1:T(8,128)(2,1)S(1)} %collective-permute-done.13), channel_id=1, source_target_pairs={{0,15},{1,0},{2,1},{3,2},{4,3},{5,4},{6,5},{7,6},{8,7},{9,8},{10,9... | collective-permute-start | bytes 294920 | tf_op jit(solution)/shard_map/ppermute | solution.py:19
  126.0 2.3 collective-permute-done.7
  128.3 4.5 %collective-permute-start.15 = (bf16[2,1,48,512]{3,2,0,1:T(8,128)(2,1)S(1)}, bf16[2,1,48,512]{3,2,0,1:T(8,128)(2,1)S(1)}, u32[]{:S(2)}, u32[]{:S(2)}) collective-permute-start(bf16[2,1,48,512]{3,2,0,1:T(8,128)(2,1)S(1)} %collective-permute-done.14), channel_id=1, source_target_pairs={{0,15},{1,0},{2,1},{3,2},{4,3},{5,4},{6,5},{7,6},{8,7},{9,8},{10,9... | collective-permute-start | bytes 294920 | tf_op jit(solution)/shard_map/ppermute | solution.py:19
  132.9 2.3 collective-permute-done.8
  137.0 4.6 %collective-permute-start.16 = (bf16[2,1,48,512]{3,2,0,1:T(8,128)(2,1)S(1)}, bf16[2,1,48,512]{3,2,0,1:T(8,128)(2,1)S(1)}, u32[]{:S(2)}, u32[]{:S(2)}) collective-permute-start(bf16[2,1,48,512]{3,2,0,1:T(8,128)(2,1)S(1)} %collective-permute-done.15), channel_id=1, source_target_pairs={{0,15},{1,0},{2,1},{3,2},{4,3},{5,4},{6,5},{7,6},{8,7},{9,8},{10,9... | collective-permute-start | bytes 294920 | tf_op jit(solution)/shard_map/ppermute | solution.py:19
  141.6 2.6 collective-permute-done.9
  151.2 3.2 collective-permute-start.17
  155.7 2.1 pad_maximum_fusion.3
  158.7 2.4 pad_maximum_fusion.2
  161.1 75.1 %all-gather.5.cloned.1.call-done = bf16[27,512,512]{2,1,0:T(8,128)(2,1)} async-done(((bf16[27,32,512]{2,1,0:T(8,128)(2,1)}), bf16[27,512,512]{2,1,0:T(8,128)(2,1)}) %all-gather.5.cloned.1.call-update) | async-done | bytes 14155792 | tf_op jit(solution)/shard_map/all_gather | solution.py:151
  256.0 30.8 %psum.30 = f32[32]{0:T(128)S(1)} all-reduce(f32[32]{0:T(128)S(1)} %reduce_sum.82), channel_id=1, replica_groups=mesh['grp'=2,'row'=16] {'row'}, use_global_device_ids=true, to_apply=%region_10.11 | all-reduce | flops 32 | bytes 256 | tf_op jit(solution)/shard_map/psum | solution.py:90
  287.3 29.5 %psum.31 = f32[32]{0:T(128)S(1)} all-reduce(f32[32]{0:T(128)S(1)} %reduce_sum.85), channel_id=1, replica_groups=mesh['grp'=2,'row'=16] {'row'}, use_global_device_ids=true, to_apply=%region_13.14 | all-reduce | flops 32 | bytes 256 | tf_op jit(solution)/shard_map/psum | solution.py:93
  (198 shorter events, 41.9 us)
Async XLA Ops:
  6.5 76.4 %copy-start = (bf16[512,512]{1,0:T(8,128)(2,1)S(1)}, bf16[512,512]{1,0:T(8,128)(2,1)}, u32[]{:S(2)}) copy-start(bf16[512,512]{1,0:T(8,128)(2,1)} %param.13) | copy-start | bytes 1572868
  6.5 78.1 %copy-start.16 = (bf16[512,512]{1,0:T(8,128)(2,1)S(1)}, bf16[512,512]{1,0:T(8,128)(2,1)}, u32[]{:S(2)}) copy-start(bf16[512,512]{1,0:T(8,128)(2,1)} %param.14) | copy-start | bytes 1572868
  6.5 128.6 %copy-start.17 = (bf16[512,512]{1,0:T(8,128)(2,1)S(1)}, bf16[512,512]{1,0:T(8,128)(2,1)}, u32[]{:S(2)}) copy-start(bf16[512,512]{1,0:T(8,128)(2,1)} %param.12) | copy-start | bytes 1572868
  6.5 140.0 %all-gather.3.cloned.1.call-start = ((), (), s32[]{:S(2)}) async-start(), calls=%async_computation | async-start | bytes 1671168 | tf_op jit(solution)/shard_map/all_gather | solution.py:128
  6.5 4.5 %collective-permute-start.1 = (bf16[2,1,48,16]{2,3,1,0:T(8,128)(2,1)}, bf16[2,1,48,16]{2,3,1,0:T(8,128)(2,1)S(1)}, u32[]{:S(2)}, u32[]{:S(2)}) collective-permute-start(bf16[2,1,48,16]{2,3,1,0:T(8,128)(2,1)} %param.9), channel_id=1, source_target_pairs={{1,0},{2,1},{3,2},{4,3},{5,4},{6,5},{7,6},{8,7},{9,8},{10,9},{11,1... | collective-permute-start | bytes 9224 | tf_op jit(solution)/shard_map/ppermute | solution.py:34
  8.0 4.1 %collective-permute-start = (bf16[2,1,48,16]{2,3,0,1:T(8,128)(2,1)}, bf16[2,1,48,16]{2,3,0,1:T(8,128)(2,1)S(1)}, u32[]{:S(2)}, u32[]{:S(2)}) collective-permute-start(bf16[2,1,48,16]{2,3,0,1:T(8,128)(2,1)} %bitcast.313), channel_id=1, source_target_pairs={{0,1},{1,2},{2,3},{3,4},{4,5},{5,6},{6,7},{7,8},{8,9},{9,10},{10,1... | collective-permute-start | bytes 9224 | tf_op jit(solution)/shard_map/ppermute | solution.py:32
  83.8 152.4 %all-gather.5.cloned.1.call-start = ((), (), s32[]{:S(2)}) async-start(), calls=%async_computation.1 | async-start | bytes 15040512 | tf_op jit(solution)/shard_map/all_gather | solution.py:151
  84.8 6.8 %collective-permute-start.2 = (bf16[2,1,48,512]{3,2,0,1:T(8,128)(2,1)S(1)}, bf16[2,1,48,512]{3,2,0,1:T(8,128)(2,1)S(1)}, u32[]{:S(2)}, u32[]{:S(2)}) collective-permute-start(bf16[2,1,48,512]{3,2,0,1:T(8,128)(2,1)S(1)} %bitcast.300), channel_id=1, source_target_pairs={{0,1},{1,2},{2,3},{3,4},{4,5},{5,6},{6,7},{7,8},{8,9},{9,10},{10,1... | collective-permute-start | bytes 294920 | tf_op jit(solution)/shard_map/ppermute | solution.py:17
  91.6 7.6 %collective-permute-start.3 = (bf16[2,1,48,512]{3,2,0,1:T(8,128)(2,1)S(1)}, bf16[2,1,48,512]{3,2,0,1:T(8,128)(2,1)S(1)}, u32[]{:S(2)}, u32[]{:S(2)}) collective-permute-start(bf16[2,1,48,512]{3,2,0,1:T(8,128)(2,1)S(1)} %collective-permute-done.2), channel_id=1, source_target_pairs={{0,1},{1,2},{2,3},{3,4},{4,5},{5,6},{6,7},{7,8},{8,9},{9,10},{10,1... | collective-permute-start | bytes 294920 | tf_op jit(solution)/shard_map/ppermute | solution.py:17
  91.6 7.6 %collective-permute-start.10 = (bf16[2,1,48,512]{3,2,0,1:T(8,128)(2,1)S(1)}, bf16[2,1,48,512]{3,2,0,1:T(8,128)(2,1)S(1)}, u32[]{:S(2)}, u32[]{:S(2)}) collective-permute-start(bf16[2,1,48,512]{3,2,0,1:T(8,128)(2,1)S(1)} %bitcast.301), channel_id=1, source_target_pairs={{0,15},{1,0},{2,1},{3,2},{4,3},{5,4},{6,5},{7,6},{8,7},{9,8},{10,9... | collective-permute-start | bytes 294920 | tf_op jit(solution)/shard_map/ppermute | solution.py:19
  99.2 6.7 %collective-permute-start.4 = (bf16[2,1,48,512]{3,2,0,1:T(8,128)(2,1)S(1)}, bf16[2,1,48,512]{3,2,0,1:T(8,128)(2,1)S(1)}, u32[]{:S(2)}, u32[]{:S(2)}) collective-permute-start(bf16[2,1,48,512]{3,2,0,1:T(8,128)(2,1)S(1)} %collective-permute-done.3), channel_id=1, source_target_pairs={{0,1},{1,2},{2,3},{3,4},{4,5},{5,6},{6,7},{7,8},{8,9},{9,10},{10,1... | collective-permute-start | bytes 294920 | tf_op jit(solution)/shard_map/ppermute | solution.py:17
  99.2 6.7 %collective-permute-start.11 = (bf16[2,1,48,512]{3,2,0,1:T(8,128)(2,1)S(1)}, bf16[2,1,48,512]{3,2,0,1:T(8,128)(2,1)S(1)}, u32[]{:S(2)}, u32[]{:S(2)}) collective-permute-start(bf16[2,1,48,512]{3,2,0,1:T(8,128)(2,1)S(1)} %collective-permute-done.10), channel_id=1, source_target_pairs={{0,15},{1,0},{2,1},{3,2},{4,3},{5,4},{6,5},{7,6},{8,7},{9,8},{10,9... | collective-permute-start | bytes 294920 | tf_op jit(solution)/shard_map/ppermute | solution.py:19
  105.9 8.7 %collective-permute-start.5 = (bf16[2,1,48,512]{3,2,0,1:T(8,128)(2,1)S(1)}, bf16[2,1,48,512]{3,2,0,1:T(8,128)(2,1)S(1)}, u32[]{:S(2)}, u32[]{:S(2)}) collective-permute-start(bf16[2,1,48,512]{3,2,0,1:T(8,128)(2,1)S(1)} %collective-permute-done.4), channel_id=1, source_target_pairs={{0,1},{1,2},{2,3},{3,4},{4,5},{5,6},{6,7},{7,8},{8,9},{9,10},{10,1... | collective-permute-start | bytes 294920 | tf_op jit(solution)/shard_map/ppermute | solution.py:17
  106.0 8.7 %collective-permute-start.12 = (bf16[2,1,48,512]{3,2,0,1:T(8,128)(2,1)S(1)}, bf16[2,1,48,512]{3,2,0,1:T(8,128)(2,1)S(1)}, u32[]{:S(2)}, u32[]{:S(2)}) collective-permute-start(bf16[2,1,48,512]{3,2,0,1:T(8,128)(2,1)S(1)} %collective-permute-done.11), channel_id=1, source_target_pairs={{0,15},{1,0},{2,1},{3,2},{4,3},{5,4},{6,5},{7,6},{8,7},{9,8},{10,9... | collective-permute-start | bytes 294920 | tf_op jit(solution)/shard_map/ppermute | solution.py:19
  114.6 6.9 %collective-permute-start.6 = (bf16[2,1,48,512]{3,2,0,1:T(8,128)(2,1)S(1)}, bf16[2,1,48,512]{3,2,0,1:T(8,128)(2,1)S(1)}, u32[]{:S(2)}, u32[]{:S(2)}) collective-permute-start(bf16[2,1,48,512]{3,2,0,1:T(8,128)(2,1)S(1)} %collective-permute-done.5), channel_id=1, source_target_pairs={{0,1},{1,2},{2,3},{3,4},{4,5},{5,6},{6,7},{7,8},{8,9},{9,10},{10,1... | collective-permute-start | bytes 294920 | tf_op jit(solution)/shard_map/ppermute | solution.py:17
  114.7 6.9 %collective-permute-start.13 = (bf16[2,1,48,512]{3,2,0,1:T(8,128)(2,1)S(1)}, bf16[2,1,48,512]{3,2,0,1:T(8,128)(2,1)S(1)}, u32[]{:S(2)}, u32[]{:S(2)}) collective-permute-start(bf16[2,1,48,512]{3,2,0,1:T(8,128)(2,1)S(1)} %collective-permute-done.12), channel_id=1, source_target_pairs={{0,15},{1,0},{2,1},{3,2},{4,3},{5,4},{6,5},{7,6},{8,7},{9,8},{10,9... | collective-permute-start | bytes 294920 | tf_op jit(solution)/shard_map/ppermute | solution.py:19
  121.6 6.7 %collective-permute-start.7 = (bf16[2,1,48,512]{3,2,0,1:T(8,128)(2,1)S(1)}, bf16[2,1,48,512]{3,2,0,1:T(8,128)(2,1)S(1)}, u32[]{:S(2)}, u32[]{:S(2)}) collective-permute-start(bf16[2,1,48,512]{3,2,0,1:T(8,128)(2,1)S(1)} %collective-permute-done.6), channel_id=1, source_target_pairs={{0,1},{1,2},{2,3},{3,4},{4,5},{5,6},{6,7},{7,8},{8,9},{9,10},{10,1... | collective-permute-start | bytes 294920 | tf_op jit(solution)/shard_map/ppermute | solution.py:17
  121.6 6.7 %collective-permute-start.14 = (bf16[2,1,48,512]{3,2,0,1:T(8,128)(2,1)S(1)}, bf16[2,1,48,512]{3,2,0,1:T(8,128)(2,1)S(1)}, u32[]{:S(2)}, u32[]{:S(2)}) collective-permute-start(bf16[2,1,48,512]{3,2,0,1:T(8,128)(2,1)S(1)} %collective-permute-done.13), channel_id=1, source_target_pairs={{0,15},{1,0},{2,1},{3,2},{4,3},{5,4},{6,5},{7,6},{8,7},{9,8},{10,9... | collective-permute-start | bytes 294920 | tf_op jit(solution)/shard_map/ppermute | solution.py:19
  128.3 6.8 %collective-permute-start.8 = (bf16[2,1,48,512]{3,2,0,1:T(8,128)(2,1)S(1)}, bf16[2,1,48,512]{3,2,0,1:T(8,128)(2,1)S(1)}, u32[]{:S(2)}, u32[]{:S(2)}) collective-permute-start(bf16[2,1,48,512]{3,2,0,1:T(8,128)(2,1)S(1)} %collective-permute-done.7), channel_id=1, source_target_pairs={{0,1},{1,2},{2,3},{3,4},{4,5},{5,6},{6,7},{7,8},{8,9},{9,10},{10,1... | collective-permute-start | bytes 294920 | tf_op jit(solution)/shard_map/ppermute | solution.py:17
  128.3 8.6 %collective-permute-start.15 = (bf16[2,1,48,512]{3,2,0,1:T(8,128)(2,1)S(1)}, bf16[2,1,48,512]{3,2,0,1:T(8,128)(2,1)S(1)}, u32[]{:S(2)}, u32[]{:S(2)}) collective-permute-start(bf16[2,1,48,512]{3,2,0,1:T(8,128)(2,1)S(1)} %collective-permute-done.14), channel_id=1, source_target_pairs={{0,15},{1,0},{2,1},{3,2},{4,3},{5,4},{6,5},{7,6},{8,7},{9,8},{10,9... | collective-permute-start | bytes 294920 | tf_op jit(solution)/shard_map/ppermute | solution.py:19
  135.2 9.0 %collective-permute-start.9 = (bf16[2,1,48,512]{3,2,0,1:T(8,128)(2,1)S(1)}, bf16[2,1,48,512]{3,2,0,1:T(8,128)(2,1)S(1)}, u32[]{:S(2)}, u32[]{:S(2)}) collective-permute-start(bf16[2,1,48,512]{3,2,0,1:T(8,128)(2,1)S(1)} %collective-permute-done.8), channel_id=1, source_target_pairs={{0,1},{1,2},{2,3},{3,4},{4,5},{5,6},{6,7},{7,8},{8,9},{9,10},{10,1... | collective-permute-start | bytes 294920 | tf_op jit(solution)/shard_map/ppermute | solution.py:17
  137.0 9.0 %collective-permute-start.16 = (bf16[2,1,48,512]{3,2,0,1:T(8,128)(2,1)S(1)}, bf16[2,1,48,512]{3,2,0,1:T(8,128)(2,1)S(1)}, u32[]{:S(2)}, u32[]{:S(2)}) collective-permute-start(bf16[2,1,48,512]{3,2,0,1:T(8,128)(2,1)S(1)} %collective-permute-done.15), channel_id=1, source_target_pairs={{0,15},{1,0},{2,1},{3,2},{4,3},{5,4},{6,5},{7,6},{8,7},{9,8},{10,9... | collective-permute-start | bytes 294920 | tf_op jit(solution)/shard_map/ppermute | solution.py:19
  149.9 4.6 %collective-permute-start.18 = (bf16[2,1,96,512]{3,2,0,1:T(8,128)(2,1)S(1)}, bf16[2,1,96,512]{3,2,0,1:T(8,128)(2,1)S(1)}, u32[]{:S(2)}, u32[]{:S(2)}) collective-permute-start(bf16[2,1,96,512]{3,2,0,1:T(8,128)(2,1)S(1)} %slice.314), channel_id=1, source_target_pairs={{1,0},{2,1},{3,2},{4,3},{5,4},{6,5},{7,6},{8,7},{9,8},{10,9},{11,1... | collective-permute-start | bytes 589832 | tf_op jit(solution)/shard_map/ppermute | solution.py:34
  151.2 4.1 %collective-permute-start.17 = (bf16[2,1,96,512]{3,2,0,1:T(8,128)(2,1)S(1)}, bf16[2,1,96,512]{3,2,0,1:T(8,128)(2,1)S(1)}, u32[]{:S(2)}, u32[]{:S(2)}) collective-permute-start(bf16[2,1,96,512]{3,2,0,1:T(8,128)(2,1)S(1)} %slice.314), channel_id=1, source_target_pairs={{0,1},{1,2},{2,3},{3,4},{4,5},{5,6},{6,7},{7,8},{8,9},{9,10},{10,1... | collective-permute-start | bytes 589832 | tf_op jit(solution)/shard_map/ppermute | solution.py:32
  (16 other events, 97.2 us)
Sparse Core Ops, SparseCore 0:
  84.0 38.9 all-gather.2
  125.1 111.0 all-gather.4
